TPU v7x, 32 devices: a whole 2x2x4 slice. The times are simulated.
32 devices in a mesh: tm: 4 (over y, core), chan: 8 (over z, x).
Axes of the slice: x: 2, y: 2, z: 4, core: 2. Of those that a mesh axis runs over, the one named last changes fastest.
Arguments:
- recordings: float32 [4, 256, 8, 512], P('tm', None, 'chan')
- gap_start: int32 [4, 256, 8], P('tm', None, 'chan'), may hold values from 0 to 511
- dropout_extent: int32 [4, 256, 8], P('tm', None, 'chan'), may hold values from 0 to 256
- filter_taps: float32 [128], replicated, may hold values from -0.5 to 0.5
- source_channel: int32 [32], P('chan'), may hold values from 0 to 255
- receiver_block: int32 [32], P('chan'), may hold values from 0 to 3
Outputs:
- stacks: float32 [128, 32, 1024], P('tm', 'chan')
All inputs are finite; a program needn't handle non-finite values.
Results may differ from a plain program's by a relative error of at most 0.0031.
Values may be sent and summed in bfloat16 or wider, within the bound.
No kernel may reach another device: no remote copies, remote signals or barrier semaphores. Data moves between devices by JAX's collectives and lax.ppermute only.
A program may use at most 64 MiB of HBM per device.

v0:
```python
import math
import jax
import jax.numpy as jnp
import numpy as np
from jax import lax
from jax.sharding import PartitionSpec as P

BLOCK = 128
MAX_LAG = 512


def passed_along(block, axis, distance):
    devices = range(lax.axis_size(axis))
    route = [(i - distance, i) for i in devices if i - distance in devices]
    return lax.ppermute(block, axis, route)


def valid_mask(starts, lengths, sample_count):
    position = jnp.arange(sample_count, dtype=jnp.int32)
    inside = (position >= starts[..., None]) & (position < starts[..., None] + lengths[..., None])
    return jnp.where(inside, 0.0, 1.0).astype(jnp.float32)


def fir_filter(signal, filter_taps):
    tap_count = filter_taps.shape[0]
    channel_count, sample_count = signal.shape
    pieces = signal.reshape(channel_count, sample_count // tap_count, tap_count)
    earlier = jnp.concatenate([jnp.zeros_like(pieces[:, :1]), pieces[:, :-1]], axis=1)
    position = jnp.arange(tap_count, dtype=jnp.int32)
    offset = position[None, :] - position[:, None]
    present_filter_tap = jnp.where(
        offset >= 0, filter_taps[jnp.clip(offset, 0, tap_count - 1)], 0.0
    )
    carried_tap = jnp.where(
        offset < 0, filter_taps[jnp.clip(offset + tap_count, 0, tap_count - 1)], 0.0
    )
    result = jnp.einsum("cki,im->ckm", pieces, present_filter_tap, precision=lax.Precision.HIGHEST)
    result = result + jnp.einsum(
        "cki,im->ckm", earlier, carried_tap, precision=lax.Precision.HIGHEST
    )
    return result.reshape(channel_count, sample_count)


def normalize_traces(filtered, retained_mask):
    counted = jnp.sum(retained_mask, axis=-1, keepdims=True)
    mean_square = jnp.sum(filtered * filtered * retained_mask, axis=-1, keepdims=True) / counted
    return (filtered * retained_mask * lax.rsqrt(mean_square + 1e-05)).astype(jnp.bfloat16)


def correlate_batch(sources, receivers, max_lag):
    sample_count = sources.shape[-1]
    tile_width = math.gcd(math.gcd(max_lag, sample_count), 128)
    tile_count = sample_count // tile_width + 1
    edge = jnp.zeros((sources.shape[0], tile_width), sources.dtype)
    source_padded = jnp.concatenate([edge, sources, edge], axis=1)
    row_table = (
        np.arange(tile_count * tile_width)[:, None] - np.arange(tile_width)[None, :] + tile_width
    )
    lag_tiles = source_padded[:, row_table]
    lag_pad = jnp.zeros((receivers.shape[0], receivers.shape[1], max_lag), receivers.dtype)
    receivers_padded = jnp.concatenate([lag_pad, receivers, lag_pad], axis=2)
    columns = []
    for lag_block in range(2 * max_lag // tile_width):
        segment_taper = receivers_padded[
            :, :, lag_block * tile_width : lag_block * tile_width + tile_count * tile_width
        ]
        columns.append(
            jnp.einsum("scz,szu->csu", segment_taper, lag_tiles, preferred_element_type=jnp.float32)
        )
    return jnp.concatenate(columns, axis=2)


def select_blocks(blocks, receiver_block, pair_count):
    picked = [
        lax.dynamic_slice_in_dim(blocks, receiver_block[pair_index], 1, axis=0)
        for pair_index in range(pair_count)
    ]
    return jnp.concatenate(picked, axis=0)


def neighbour_blocks(owned_rows):
    return passed_along(owned_rows, "chan", -1)


def local(recordings, gap_start, dropout_extent, filter_taps, source_channel, receiver_block):
    traces = recordings[0, :, 0, :]
    retained_mask = valid_mask(gap_start[0, :, 0], dropout_extent[0, :, 0], traces.shape[1])
    filtered = fir_filter(traces * retained_mask, filter_taps)
    normalized = normalize_traces(filtered, retained_mask)
    round_count, sample_count = normalized.shape
    regrouped = lax.all_to_all(
        normalized.reshape(round_count, 1, sample_count),
        "chan",
        split_axis=0,
        concat_axis=1,
        tiled=True,
    )
    owned_rows = regrouped.reshape(round_count, sample_count)
    sources = owned_rows[source_channel]
    segment_count = lax.axis_size("tm")
    factor = 1.0 / math.sqrt(sample_count * segment_count)
    pair_count = sources.shape[0]
    block_count = round_count // BLOCK
    following = neighbour_blocks(owned_rows)
    blocks = jnp.concatenate([owned_rows, following], axis=0).reshape(
        2 * block_count, BLOCK, sample_count
    )
    receivers = select_blocks(blocks, receiver_block, pair_count)
    stack_terms = correlate_batch(sources, receivers, MAX_LAG) * factor
    stacks = lax.psum_scatter(stack_terms, "tm", scatter_dimension=0, tiled=True)
    return stacks


def solution(mesh):
    return jax.shard_map(
        local,
        mesh=mesh,
        in_specs=(
            P("tm", None, "chan", None),
            P("tm", None, "chan"),
            P("tm", None, "chan"),
            P(),
            P("chan"),
            P("chan"),
        ),
        out_specs=P("tm", "chan", None),
        check_vma=False,
    )
```

profile of v0, /device:TPU:0, one launch (start us, length us, event | category | flops | bytes accessed | tf_op | source)
XLA Modules:
  0.0 605.1 jit_solution(15314912430270999718)
XLA Ops:
  6.5 0.0 copy-start
  6.6 1.2 copy.46
  7.9 0.0 copy-done
  7.9 97.2 %gather_fusion = f32[16384]{0:T(1024)S(1)} fusion(f32[128]{0:T(128)S(1)} %copy-done, s32[16384]{0:T(1024)S(1)} %fusion.21), kind=kCustom, calls=%fused_computation | custom fusion | bytes 196608 | tf_op jit(solution)/shard_map/gather | solution.py:32
  105.1 0.0 copy-start.2
  105.1 0.0 copy-start.4
  105.1 97.2 %gather_fusion.1 = f32[16384]{0:T(1024)S(1)} fusion(f32[128]{0:T(128)S(1)} %copy-done, s32[16384]{0:T(1024)S(1)} %fusion.23), kind=kCustom, calls=%fused_computation.1 | custom fusion | bytes 196608 | tf_op jit(solution)/shard_map/gather | solution.py:35
  202.3 0.0 copy-done.2
  202.3 0.0 copy-done.4
  202.4 0.2 select_reduce_fusion
  202.6 0.2 select_multiply_fusion.1
  202.8 0.6 fusion.25
  203.4 0.0 copy-start.1
  203.4 0.7 fusion.16
  204.2 0.2 copy.63
  204.4 0.2 multiply_convert_fusion
  204.6 0.5 broadcast.235
  205.1 0.8 reduce.1
  205.9 0.9 reshape.270
  206.8 7.2 %all-to-all-start = ((bf16[8,2,8192]{2,1,0:T(2,128)(2,1)}), bf16[8,2,8192]{2,1,0:T(2,128)(2,1)S(1)}, u32[]{:S(2)}, u32[]{:S(2)}) async-start(bf16[8,2,8192]{2,1,0:T(2,128)(2,1)} %reshape.270), calls=%async_computation | async-start | bytes 524288 | tf_op jit(solution)/shard_map/all_to_all | solution.py:91
  214.0 0.0 all-reduce.6.cloned.1.call-start
  214.2 8.8 %all-to-all-done = bf16[8,2,8192]{2,1,0:T(2,128)(2,1)S(1)} async-done(((bf16[8,2,8192]{2,1,0:T(2,128)(2,1)}), bf16[8,2,8192]{2,1,0:T(2,128)(2,1)S(1)}, u32[]{:S(2)}, u32[]{:S(2)}) %all-to-all-start) | async-done | bytes 262176 | tf_op jit(solution)/shard_map/all_to_all | solution.py:91
  223.0 0.3 reshape.271
  223.3 0.2 copy.66
  223.4 1.3 collective-permute-start
  224.7 0.0 copy-done.3
  224.8 0.7 fusion.47
  233.0 0.6 gather_fusion.2
  233.6 0.2 copy.54
  233.8 286.2 %gather_fusion.3 = bf16[81920,4]{1,0:T(8,128)(2,1)} fusion(bf16[4,768]{0,1:T(8,128)(2,1)S(1)} %copy.54, s32[81920]{0:T(1024)S(1)} %broadcast_clamp_fusion), kind=kCustom, calls=%fused_computation.3 | custom fusion | bytes 1638400 | tf_op jit(solution)/shard_map/gather | solution.py:59
  520.0 19.5 %copy.55 = bf16[640,128,4]{0,1,2:T(8,128)(2,1)S(1)} copy(bf16[640,128,4]{2,1,0:T(8,128)(2,1)} %bitcast.95) | data formatting | bytes 1310720 | tf_op jit(solution)/shard_map/gather | solution.py:59
  539.5 0.0 collective-permute-done
  539.6 0.1 pad_maximum_fusion.1
  539.6 0.3 fusion.7
  540.0 0.3 fusion.6
  540.3 0.3 fusion.5
  540.6 0.4 fusion.4
  541.0 0.4 fusion.3
  541.4 0.3 fusion.2
  541.7 0.3 fusion.1
  542.1 0.3 fusion
  542.4 0.2 broadcast_multiply_fusion
  542.6 2.0 copy.56
  544.6 0.0 all-reduce.6.cloned.1.call-update
  544.7 0.6 copy-done.6
  545.3 0.6 dynamic-slice
  546.5 49.9 %all-reduce.6.cloned.1.call-done = f32[128,4,1024]{2,1,0:T(4,128)} async-done(((f32[128,4,1024]{2,1,0:T(4,128)}), f32[128,4,1024]{2,1,0:T(4,128)}) %all-reduce.6.cloned.1.call-update) | async-done | bytes 2097168
  596.4 1.9 constant_dynamic-slice_fusion.4
  (18 shorter events, 0.3 us)
Async XLA Ops:
  6.5 1.3 copy-start
  105.1 97.2 %copy-start.2 = (s32[1,256,1]{1,2,0:T(1,128)S(1)}, s32[1,256,1]{1,2,0:T(1,128)}, u32[]{:S(2)}) copy-start(s32[1,256,1]{1,2,0:T(1,128)} %param.9) | copy-start | bytes 3076
  105.1 97.2 %copy-start.4 = (s32[1,256,1]{1,2,0:T(1,128)S(1)}, s32[1,256,1]{1,2,0:T(1,128)}, u32[]{:S(2)}) copy-start(s32[1,256,1]{1,2,0:T(1,128)} %param.10) | copy-start | bytes 3076
  203.4 10.7 %copy-start.1 = (s32[81920]{0:T(1024)S(1)}, s32[81920]{0:T(1024)}, u32[]{:S(2)}) copy-start(s32[81920]{0:T(1024)} %constant.48) | copy-start | bytes 983044
  204.2 10.0 %copy-start.5 = (s32[4]{0:T(128)S(1)}, s32[4]{0:T(128)}, u32[]{:S(2)}) copy-start(s32[4]{0:T(128)} %param.12) | copy-start | bytes 52
  205.1 19.6 %copy-start.3 = (s32[4]{0:T(128)S(1)}, s32[4]{0:T(128)}, u32[]{:S(2)}) copy-start(s32[4]{0:T(128)} %param.13) | copy-start | bytes 52
  206.8 16.2 %all-to-all-start = ((bf16[8,2,8192]{2,1,0:T(2,128)(2,1)}), bf16[8,2,8192]{2,1,0:T(2,128)(2,1)S(1)}, u32[]{:S(2)}, u32[]{:S(2)}) async-start(bf16[8,2,8192]{2,1,0:T(2,128)(2,1)} %reshape.270), calls=%async_computation | async-start | bytes 524288 | tf_op jit(solution)/shard_map/all_to_all | solution.py:91
  214.0 382.4 %all-reduce.6.cloned.1.call-start = ((), (), s32[]{:S(2)}) async-start(), calls=%async_computation.1 | async-start | bytes 4194304
  223.4 316.0 %collective-permute-start = (bf16[256,512]{1,0:T(8,128)(2,1)S(1)}, bf16[256,512]{1,0:T(8,128)(2,1)S(1)}, u32[]{:S(2)}, u32[]{:S(2)}) collective-permute-start(bf16[256,512]{1,0:T(8,128)(2,1)S(1)} %bitcast.99), channel_id=1, source_target_pairs={{1,0},{2,1},{3,2},{4,3},{5,4},{6,5},{7,6},{9,8},{10,9},{11,10},{12... | collective-permute-start | bytes 786440 | tf_op jit(solution)/shard_map/ppermute | solution.py:15
  544.6 0.7 copy-start.6
Sparse Core Ops, SparseCore 0:
  544.8 51.5 all-reduce.5
where the time goes:
time: 606 us; the launch traced here: 605 us
  local copies, waits for them, and re-layouts  510 us (84%)
  waiting for transfers between devices  58.7 us (10%)
  between operations  21.9 us (4%)
  starting transfers between devices  8.58 us (1%)
    gather x2, local copies, waits for them, and re-layouts, correlate_batch(): lag_tiles = source_padded[:, row_table]  306 us
    gather x1, local copies, waits for them, and re-layouts, fir_filter(): filter_taps[jnp.clip(offset, 0, tap_count - 1)]  97.2 us
    gather x1, local copies, waits for them, and re-layouts, fir_filter(): filter_taps[jnp.clip(offset + tap_count, 0, tap_count - 1)]  97.2 us
    unnamed x2, waiting for transfers between devices  49.9 us
  transfers between devices with their start and end apart: 3, of which 2 were waited for; matrix products, arithmetic and copies ran while one was open for 51% of the time, Pallas kernels for 0%

commit v1 on v0

--- a/solution.py
+++ b/solution.py
@@ -88,13 +88,19 @@
     filtered = fir_filter(traces * retained_mask, filter_taps)
     normalized = normalize_traces(filtered, retained_mask)
     round_count, sample_count = normalized.shape
-    regrouped = lax.all_to_all(
-        normalized.reshape(round_count, 1, sample_count),
-        "chan",
-        split_axis=0,
-        concat_axis=1,
-        tiled=True,
-    )
+    x = normalized.reshape(round_count, 1, sample_count)
+    ways, here = (lax.axis_size("chan"), lax.axis_index("chan"))
+    width = x.shape[0] // ways
+    dims = list(x.shape)
+    dims[0] = width
+    height = dims[1]
+    dims[1] = height * ways
+    regrouped = jnp.zeros(dims, x.dtype)
+    for mask in range(ways):
+        part = lax.dynamic_slice_in_dim(x, (here ^ mask) * width, width, axis=0)
+        if mask:
+            part = lax.ppermute(part, "chan", [(d, d ^ mask) for d in range(ways)])
+        regrouped = lax.dynamic_update_slice_in_dim(regrouped, part, (here ^ mask) * height, axis=1)
     owned_rows = regrouped.reshape(round_count, sample_count)
     sources = owned_rows[source_channel]
     segment_count = lax.axis_size("tm")

time: 606 us -> 605 us (level)
  waiting for transfers between devices: 58.7 us -> 52.3 us
    ppermute x0 -> x7, starting transfers between devices: none -> 12.6 us  [local(): part = lax.ppermute(part, 'chan', [(d, d ^ mask) for d in range(ways)])]
    all_to_all x1 -> x0, waiting for transfers between devices: 8.79 us -> none  [local(): lax.all_to_all(normalized.reshape(round_count, 1, sample_count), 'chan',...]
    all_to_all x1 -> x0, starting transfers between devices: 7.25 us -> none  [local(): lax.all_to_all(normalized.reshape(round_count, 1, sample_count), 'chan',...]
  transfers between devices with their start and end apart: 3 -> 9, of which waited for: 2 -> 2; matrix products, arithmetic and copies ran while one was open for 51% -> 51% of each run, Pallas kernels for 0% -> 0%
where the time goes in v1:
time: 605 us
  local copies, waits for them, and re-layouts  511 us (84%)
  waiting for transfers between devices  52.3 us (9%)
  between operations  22 us (4%)
  starting transfers between devices  13.9 us (2%)
    gather x2, local copies, waits for them, and re-layouts, correlate_batch(): lag_tiles = source_padded[:, row_table]  304 us
    gather x1, local copies, waits for them, and re-layouts, fir_filter(): filter_taps[jnp.clip(offset + tap_count, 0, tap_count - 1)]  97.2 us
    gather x1, local copies, waits for them, and re-layouts, fir_filter(): filter_taps[jnp.clip(offset, 0, tap_count - 1)]  97.2 us
    unnamed x2, waiting for transfers between devices  50.5 us
    ppermute x7, starting transfers between devices, local(): part = lax.ppermute(part, 'chan', [(d, d ^ mask) for d in range(ways)])  12.6 us
  transfers between devices with their start and end apart: 9, of which 2 were waited for; matrix products, arithmetic and copies ran while one was open for 51% of the time, Pallas kernels for 0%

profile of v1, /device:TPU:0, one launch (start us, length us, event | category | flops | bytes accessed | tf_op | source)
XLA Modules:
  0.0 604.6 jit_solution(15951015988526309096)
XLA Ops:
  6.7 1.2 copy.32
  7.9 97.2 %gather_fusion = f32[16384]{0:T(1024)S(1)} fusion(f32[128]{0:T(128)S(1)} %copy-done, s32[16384]{0:T(1024)S(1)} %fusion.22), kind=kCustom, calls=%fused_computation | custom fusion | bytes 196608 | tf_op jit(solution)/shard_map/gather | solution.py:32
  105.2 97.2 %gather_fusion.1 = f32[16384]{0:T(1024)S(1)} fusion(f32[128]{0:T(128)S(1)} %copy-done, s32[16384]{0:T(1024)S(1)} %fusion.24), kind=kCustom, calls=%fused_computation.1 | custom fusion | bytes 196608 | tf_op jit(solution)/shard_map/gather | solution.py:35
  202.4 0.2 select_reduce_fusion
  202.6 0.2 select_multiply_fusion.2
  202.8 0.6 fusion.26
  203.5 0.7 fusion.16
  204.2 0.2 copy.37
  204.4 0.2 fusion.18
  204.7 3.0 collective-permute-start
  207.7 1.6 collective-permute-start.1
  209.3 3.0 collective-permute-start.3
  212.3 1.3 collective-permute-start.4
  213.7 3.7 collective-permute-start.5
  217.3 0.1 collective-permute-start.6
  217.5 0.6 dynamic_update_slice.24
  218.1 0.1 copy.39
  218.2 0.6 dynamic_update_slice.25
  218.8 0.1 copy.40
  218.9 0.6 dynamic_update_slice.26
  219.5 0.1 copy.41
  219.5 0.6 dynamic_update_slice.27
  220.2 0.6 dynamic_update_slice.28
  220.9 0.6 dynamic_update_slice.29
  221.6 0.6 dynamic_update_slice.30
  222.2 1.7 collective-permute-done.6
  224.0 0.6 dynamic_update_slice.31
  224.6 1.3 collective-permute-start.7
  225.9 0.6 fusion.48
  234.0 0.6 gather_fusion.2
  234.5 0.2 copy.46
  234.7 284.2 %gather_fusion.3 = bf16[81920,4]{1,0:T(8,128)(2,1)} fusion(bf16[4,768]{0,1:T(8,128)(2,1)S(1)} %copy.46, s32[81920]{0:T(1024)S(1)} %broadcast_clamp_fusion), kind=kCustom, calls=%fused_computation.3 | custom fusion | bytes 1638400 | tf_op jit(solution)/shard_map/gather | solution.py:59
  518.9 19.5 %copy.47 = bf16[640,128,4]{0,1,2:T(8,128)(2,1)S(1)} copy(bf16[640,128,4]{2,1,0:T(8,128)(2,1)} %bitcast.106) | data formatting | bytes 1310720 | tf_op jit(solution)/shard_map/gather | solution.py:59
  538.5 0.1 pad_maximum_fusion.1
  538.6 0.3 fusion.7
  538.9 0.3 fusion.6
  539.2 0.3 fusion.5
  539.5 0.4 fusion.4
  539.9 0.4 fusion.3
  540.3 0.3 fusion.2
  540.7 0.3 fusion.1
  541.0 0.3 fusion
  541.3 0.2 broadcast_multiply_fusion
  541.5 2.0 copy.48
  543.6 0.6 copy-done.6
  544.2 0.6 dynamic-slice.32
  545.4 50.5 %all-reduce.6.cloned.1.call-done = f32[128,4,1024]{2,1,0:T(4,128)} async-done(((f32[128,4,1024]{2,1,0:T(4,128)}), f32[128,4,1024]{2,1,0:T(4,128)}) %all-reduce.6.cloned.1.call-update) | async-done | bytes 2097168
  595.9 1.9 constant_dynamic-slice_fusion.4
  (42 shorter events, 0.6 us)
Async XLA Ops:
  6.5 1.4 copy-start
  6.5 589.4 %all-reduce.6.cloned.1.call-start = ((), (), s32[]{:S(2)}) async-start(), calls=%async_computation | async-start | bytes 4194304
  105.1 97.2 %copy-start.2 = (s32[1,256,1]{1,2,0:T(1,128)S(1)}, s32[1,256,1]{1,2,0:T(1,128)}, u32[]{:S(2)}) copy-start(s32[1,256,1]{1,2,0:T(1,128)} %param.9) | copy-start | bytes 3076
  105.2 97.2 %copy-start.4 = (s32[1,256,1]{1,2,0:T(1,128)S(1)}, s32[1,256,1]{1,2,0:T(1,128)}, u32[]{:S(2)}) copy-start(s32[1,256,1]{1,2,0:T(1,128)} %param.10) | copy-start | bytes 3076
  203.4 10.2 %copy-start.1 = (s32[81920]{0:T(1024)S(1)}, s32[81920]{0:T(1024)}, u32[]{:S(2)}) copy-start(s32[81920]{0:T(1024)} %constant.70) | copy-start | bytes 983044
  203.5 13.9 %copy-start.5 = (s32[4]{0:T(128)S(1)}, s32[4]{0:T(128)}, u32[]{:S(2)}) copy-start(s32[4]{0:T(128)} %param.12) | copy-start | bytes 52
  204.4 21.5 %copy-start.3 = (s32[4]{0:T(128)S(1)}, s32[4]{0:T(128)}, u32[]{:S(2)}) copy-start(s32[4]{0:T(128)} %param.13) | copy-start | bytes 52
  204.7 8.9 %collective-permute-start = (bf16[32,1,512]{2,0,1:T(8,128)(2,1)S(1)}, bf16[32,1,512]{2,0,1:T(8,128)(2,1)S(1)}, u32[]{:S(2)}, u32[]{:S(2)}) collective-permute-start(bf16[32,1,512]{2,0,1:T(8,128)(2,1)S(1)} %get-tuple-element.15), channel_id=1, source_target_pairs={{0,1},{1,0},{2,3},{3,2},{4,5},{5,4},{6,7},{7,6},{8,9},{9,8},{10,11... | collective-permute-start | bytes 98312 | tf_op jit(solution)/shard_map/ppermute | solution.py:102
  207.7 9.6 %collective-permute-start.1 = (bf16[32,1,512]{2,0,1:T(8,128)(2,1)S(1)}, bf16[32,1,512]{2,0,1:T(8,128)(2,1)S(1)}, u32[]{:S(2)}, u32[]{:S(2)}) collective-permute-start(bf16[32,1,512]{2,0,1:T(8,128)(2,1)S(1)} %get-tuple-element.14), channel_id=1, source_target_pairs={{0,2},{1,3},{2,0},{3,1},{4,6},{5,7},{6,4},{7,5},{8,10},{9,11},{10,... | collective-permute-start | bytes 98312 | tf_op jit(solution)/shard_map/ppermute | solution.py:102
  209.3 10.2 %collective-permute-start.2 = (bf16[32,1,512]{2,0,1:T(8,128)(2,1)S(1)}, bf16[32,1,512]{2,0,1:T(8,128)(2,1)S(1)}, u32[]{:S(2)}, u32[]{:S(2)}) collective-permute-start(bf16[32,1,512]{2,0,1:T(8,128)(2,1)S(1)} %get-tuple-element.13), channel_id=1, source_target_pairs={{0,3},{1,2},{2,1},{3,0},{4,7},{5,6},{6,5},{7,4},{8,11},{9,10},{10,... | collective-permute-start | bytes 98312 | tf_op jit(solution)/shard_map/ppermute | solution.py:102
  209.3 10.8 %collective-permute-start.3 = (bf16[32,1,512]{2,0,1:T(8,128)(2,1)S(1)}, bf16[32,1,512]{2,0,1:T(8,128)(2,1)S(1)}, u32[]{:S(2)}, u32[]{:S(2)}) collective-permute-start(bf16[32,1,512]{2,0,1:T(8,128)(2,1)S(1)} %get-tuple-element.12), channel_id=1, source_target_pairs={{0,4},{1,5},{2,6},{3,7},{4,0},{5,1},{6,2},{7,3},{8,12},{9,13},{10,... | collective-permute-start | bytes 98312 | tf_op jit(solution)/shard_map/ppermute | solution.py:102
  212.3 8.5 %collective-permute-start.4 = (bf16[32,1,512]{2,0,1:T(8,128)(2,1)S(1)}, bf16[32,1,512]{2,0,1:T(8,128)(2,1)S(1)}, u32[]{:S(2)}, u32[]{:S(2)}) collective-permute-start(bf16[32,1,512]{2,0,1:T(8,128)(2,1)S(1)} %get-tuple-element.11), channel_id=1, source_target_pairs={{0,5},{1,4},{2,7},{3,6},{4,1},{5,0},{6,3},{7,2},{8,13},{9,12},{10,... | collective-permute-start | bytes 98312 | tf_op jit(solution)/shard_map/ppermute | solution.py:102
  213.7 7.9 %collective-permute-start.5 = (bf16[32,1,512]{2,0,1:T(8,128)(2,1)S(1)}, bf16[32,1,512]{2,0,1:T(8,128)(2,1)S(1)}, u32[]{:S(2)}, u32[]{:S(2)}) collective-permute-start(bf16[32,1,512]{2,0,1:T(8,128)(2,1)S(1)} %get-tuple-element.10), channel_id=1, source_target_pairs={{0,6},{1,7},{2,4},{3,5},{4,2},{5,3},{6,0},{7,1},{8,14},{9,15},{10,... | collective-permute-start | bytes 98312 | tf_op jit(solution)/shard_map/ppermute | solution.py:102
  217.3 6.6 %collective-permute-start.6 = (bf16[32,1,512]{2,0,1:T(8,128)(2,1)S(1)}, bf16[32,1,512]{2,0,1:T(8,128)(2,1)S(1)}, u32[]{:S(2)}, u32[]{:S(2)}) collective-permute-start(bf16[32,1,512]{2,0,1:T(8,128)(2,1)S(1)} %get-tuple-element.9), channel_id=1, source_target_pairs={{0,7},{1,6},{2,5},{3,4},{4,3},{5,2},{6,1},{7,0},{8,15},{9,14},{10,... | collective-permute-start | bytes 98312 | tf_op jit(solution)/shard_map/ppermute | solution.py:102
  224.6 313.8 %collective-permute-start.7 = (bf16[256,512]{1,0:T(8,128)(2,1)S(1)}, bf16[256,512]{1,0:T(8,128)(2,1)S(1)}, u32[]{:S(2)}, u32[]{:S(2)}) collective-permute-start(bf16[256,512]{1,0:T(8,128)(2,1)S(1)} %bitcast.110), channel_id=1, source_target_pairs={{1,0},{2,1},{3,2},{4,3},{5,4},{6,5},{7,6},{9,8},{10,9},{11,10},{12... | collective-permute-start | bytes 786440 | tf_op jit(solution)/shard_map/ppermute | solution.py:15
  543.6 0.7 copy-start.6
Sparse Core Ops, SparseCore 0:
  543.7 52.1 all-reduce.5
